TPU v7x, 32 devices: a whole 2x2x4 slice. The times are simulated.
32 devices in a mesh: section: 4 (over z), row: 8 (over y, x, core).
Axes of the slice: x: 2, y: 2, z: 4, core: 2. Of those that a mesh axis runs over, the one named last changes fastest.
Arguments:
- features: bfloat16 [16, 16, 16, 192], P(None, 'row'), may hold values from -6 to 6
- norm_gain: float32 [4, 192], P('section'), may hold values from 0.5 to 1.5
- conv_weight: bfloat16 [4, 3, 3, 3, 192, 192], P('section'), may hold values from -0.078125 to 0.078125
- conv_bias: float32 [4, 192], P('section'), may hold values from -2.5 to 2.5
Outputs:
- decoded: bfloat16 [16, 16, 16, 192], P('section', 'row')
All inputs are finite; a program needn't handle non-finite values.
Results may differ from a plain program's by a relative error of at most 0.03.
Values may be sent and summed in bfloat16 or wider, within the bound.
A program may use at most 64 MiB of HBM per device.

v0:
```python
import jax
import jax.numpy as jnp
from jax import lax
from jax.sharding import PartitionSpec as P

FRAMES = 4


def with_halo(block, sides, width):
    for axis, dim in sides:
        count = lax.axis_size(axis)
        forward = [(i, i + 1) for i in range(count - 1)]
        backward = [(target, source) for source, target in forward]
        low = lax.ppermute(
            lax.slice_in_dim(block, block.shape[dim] - width, None, axis=dim), axis, forward
        )
        high = lax.ppermute(lax.slice_in_dim(block, 0, width, axis=dim), axis, backward)
        block = jnp.concatenate([low, block, high], axis=dim)
    return block


def shifted(value, axis, steps):
    count = lax.axis_size(axis)
    first, last = (max(0, -steps), min(count, count - steps))
    return lax.ppermute(value, axis, [(source, source + steps) for source in range(first, last)])


def on_device(features, norm_gain, conv_weight, conv_bias):
    sections = lax.axis_size("section")
    place = lax.axis_index("section")
    frames_all, rows_dev, cols, chans = features.shape
    group = 2
    span = group * FRAMES
    batches = sections // group
    turns = batches + sections - 1
    blocks = features.reshape(batches, span, rows_dev, cols, chans)
    gain = norm_gain[0]
    bias = conv_bias[0]
    taps = conv_weight[0].reshape(3, 9 * chans, chans)

    def activate(state):
        wide = state.astype(jnp.float32)
        square = jnp.mean(wide * wide, axis=-1, keepdims=True)
        return jax.nn.silu(wide * lax.rsqrt(square + 1e-06) * gain).astype(jnp.bfloat16)

    def convolve(padded, state):
        framed = jnp.pad(padded, ((0, 0), (0, 0), (1, 1), (0, 0)))
        total = jnp.zeros((span * rows_dev * cols, chans), jnp.float32)
        for delay in range(3):
            window = framed[delay : delay + span]
            pieces = [
                window[:, dy : dy + rows_dev, dx : dx + cols] for dy in range(3) for dx in range(3)
            ]
            stacked = jnp.concatenate(pieces, axis=-1).reshape(-1, 9 * chans)
            total = total + jnp.dot(stacked, taps[delay], preferred_element_type=jnp.float32)
        result = state.astype(jnp.float32) + total.reshape(span, rows_dev, cols, chans) + bias
        return result.astype(jnp.bfloat16)

    memory = jnp.zeros((2, rows_dev, cols, chans), jnp.bfloat16)
    incoming = jnp.zeros((span, rows_dev, cols, chans), jnp.bfloat16)
    finished = jnp.zeros((batches, span, rows_dev, cols, chans), jnp.bfloat16)

    def advance(carry, turn):
        incoming, memory, finished = carry
        batch = turn - place
        active = jnp.logical_and(batch >= 0, batch < batches)
        slot = jnp.clip(batch, 0, batches - 1)
        own = lax.dynamic_index_in_dim(blocks, jnp.clip(turn, 0, batches - 1), 0, keepdims=False)
        state = jnp.where(place == 0, own, incoming)
        normed = activate(state)
        joined = jnp.concatenate([memory, normed], axis=0)
        padded = with_halo(joined, (("row", 1),), 1)
        renewed = normed[-2:]
        memory = jnp.where(active, renewed, memory)
        output = lax.cond(active, lambda: convolve(padded, state), lambda: state)
        keeping = jnp.logical_and(active, place == sections - 1)
        finished = jnp.where(
            keeping, lax.dynamic_update_index_in_dim(finished, output, slot, 0), finished
        )
        incoming = shifted(output, "section", 1)
        return ((incoming, memory, finished), None)

    carry, unused = lax.scan(advance, (incoming, memory, finished), jnp.arange(turns))
    finished = carry[2].reshape(sections, 1, FRAMES, rows_dev, cols, chans)
    received = lax.all_to_all(finished, "section", split_axis=0, concat_axis=1, tiled=True)
    return received[0, sections - 1]


def solution(mesh):
    in_specs = (
        P(None, "row", None, None),
        P("section", None),
        P("section", None, None, None, None, None),
        P("section", None),
    )
    out_specs = P("section", "row", None, None)
    return jax.shard_map(
        on_device, mesh=mesh, in_specs=in_specs, out_specs=out_specs, check_vma=False
    )
```

profile of v0, /device:TPU:2, one launch (start us, length us, event | category | flops | bytes accessed | tf_op | source)
XLA Modules:
  0.0 166.4 jit_solution(8224347381871252293)
XLA Ops:
  0.7 140.7 %while.16 = (s32[]{:T(128)}, bf16[8,2,16,192]{3,2,1,0:T(8,128)(2,1)S(1)}, bf16[2,2,16,192]{3,2,1,0:T(8,128)(2,1)}, bf16[2,8,2,16,192]{4,3,2,1,0:T(8,128)(2,1)}, ...) while((s32[]{:T(128)}, ...), condition=%wide.region_4.5_spmd.clone, body=%wide.region_0.4_spmd.clone.sunk | while | flops 510996736 | bytes 19456960 | solution.py:83
  5.2 1.9 %collective-permute-start = (bf16[10,1,16,192]{3,2,1,0:T(8,128)(2,1)S(1)}, bf16[10,1,16,192]{3,2,1,0:T(8,128)(2,1)S(1)}, u32[]{:S(2)}, u32[]{:S(2)}) collective-permute-start(bf16[10,1,16,192]{3,2,1,0:T(8,128)(2,1)S(1)} %get-tuple-element.311), channel_id=1, source_target_pairs={{1,0},{2,1},{3,2},{4,3},{5,4},{6,5},{7,6},{9,8},{10,9},{11,10},{12... | collective-permute-start | bytes 184328 | tf_op jit(solution)/shard_map/while/body/eval_jaxpr/ppermute | solution.py:17
  7.1 2.4 %collective-permute-start.1 = (bf16[10,1,16,192]{3,2,1,0:T(8,128)(2,1)S(1)}, bf16[10,1,16,192]{3,2,1,0:T(8,128)(2,1)S(1)}, u32[]{:S(2)}, u32[]{:S(2)}) collective-permute-start(bf16[10,1,16,192]{3,2,1,0:T(8,128)(2,1)S(1)} %get-tuple-element.312), channel_id=1, source_target_pairs={{0,1},{1,2},{2,3},{3,4},{4,5},{5,6},{6,7},{8,9},{9,10},{10,11},{11... | collective-permute-start | bytes 184328 | tf_op jit(solution)/shard_map/while/body/eval_jaxpr/ppermute | solution.py:14
  9.6 3.3 %collective-permute-done.1 = bf16[10,1,16,192]{3,2,1,0:T(8,128)(2,1)S(1)} collective-permute-done((bf16[10,1,16,192]{3,2,1,0:T(8,128)(2,1)S(1)}, bf16[10,1,16,192]{3,2,1,0:T(8,128)(2,1)S(1)}, u32[]{:S(2)}, u32[]{:S(2)}) %collective-permute-start.1) | collective-permute-done | bytes 61472 | tf_op jit(solution)/shard_map/while/body/eval_jaxpr/ppermute | solution.py:14
  13.0 10.9 %conditional.3 = (bf16[8,2,16,192]{3,2,1,0:T(8,128)(2,1)S(1)}) conditional(s32[]{:T(128)} %convert_element_type.53, bf16[8,2,16,192]{3,2,1,0:T(8,128)(2,1)S(1)} %get-tuple-element.308, (bf16[8,2,16,192]{3,2,1,0:T(8,128)(2,1)S(1)}, bf16[10,4,16,192]{3,2,1,0:T(8,128)(2,1)S(1)}, bf16[3,1728,192]{2,1,0:T(8,128)(2,1)}, f32[1,192]{1,0:T(1,128)}) %tuple.80), branch_computations={%region_2.2_spmd, %region_3.3_spmd} | conditional | flops 509902848 | bytes 16879396 | solution.py:75
  13.1 1.4 pad_slice_fusion
  14.5 1.3 concatenate.14
  15.8 1.4 concatenate.12
  17.2 1.7 %fusion.2 = f32[256,192]{0,1:T(8,128)S(1)} fusion(bf16[256,1728]{1,0:T(8,128)(2,1)S(1)} %bitcast.40, bf16[3,1728,192]{2,1,0:T(8,128)(2,1)} %get-tuple-element.112), kind=kOutput, calls=%fused_computation.22 | convolution fusion | flops 169869312 | bytes 1966080 | tf_op jit(solution)/shard_map/while/body/eval_jaxpr/cond/branch_1_fun/dot_general | solution.py:55
  20.3 1.7 %convolution_add_fusion.1 = f32[256,192]{0,1:T(8,128)S(1)} fusion(f32[256,192]{0,1:T(8,128)S(1)} %fusion.2, bf16[256,1728]{1,0:T(8,128)(2,1)S(1)} %bitcast.39, bf16[3,1728,192]{2,1,0:T(8,128)(2,1)} %get-tuple-element.112), kind=kOutput, calls=%fused_computation.1 | convolution fusion | flops 169918464 | bytes 2162688 | tf_op jit(solution)/shard_map/while/body/eval_jaxpr/cond/branch_1_fun/dot_general | solution.py:55
  22.0 1.7 %convolution_add_fusion = f32[256,192]{0,1:T(8,128)S(1)} fusion(f32[256,192]{0,1:T(8,128)S(1)} %convolution_add_fusion.1, bf16[256,1728]{1,0:T(8,128)(2,1)S(1)} %bitcast.38, bf16[3,1728,192]{2,1,0:T(8,128)(2,1)} %get-tuple-element.112), kind=kOutput, calls=%fused_computation | convolution fusion | flops 169918464 | bytes 2162688 | tf_op jit(solution)/shard_map/while/body/eval_jaxpr/cond/branch_1_fun/dot_general | solution.py:55
  25.2 1.6 fusion.28
  26.8 1.7 %collective-permute-done.2 = bf16[8,2,16,192]{3,2,1,0:T(8,128)(2,1)S(1)} collective-permute-done((bf16[8,2,16,192]{3,2,1,0:T(8,128)(2,1)S(1)}, bf16[8,2,16,192]{3,2,1,0:T(8,128)(2,1)S(1)}, u32[]{:S(2)}, u32[]{:S(2)}) %collective-permute-start.2) | collective-permute-done | bytes 98336 | tf_op jit(solution)/shard_map/while/body/eval_jaxpr/ppermute | solution.py:25
  32.2 1.4 slice_select_fusion.2
  33.7 1.9 %collective-permute-start = (bf16[10,1,16,192]{3,2,1,0:T(8,128)(2,1)S(1)}, bf16[10,1,16,192]{3,2,1,0:T(8,128)(2,1)S(1)}, u32[]{:S(2)}, u32[]{:S(2)}) collective-permute-start(bf16[10,1,16,192]{3,2,1,0:T(8,128)(2,1)S(1)} %get-tuple-element.311), channel_id=1, source_target_pairs={{1,0},{2,1},{3,2},{4,3},{5,4},{6,5},{7,6},{9,8},{10,9},{11,10},{12... | collective-permute-start | bytes 184328 | tf_op jit(solution)/shard_map/while/body/eval_jaxpr/ppermute | solution.py:17
  35.6 2.4 %collective-permute-start.1 = (bf16[10,1,16,192]{3,2,1,0:T(8,128)(2,1)S(1)}, bf16[10,1,16,192]{3,2,1,0:T(8,128)(2,1)S(1)}, u32[]{:S(2)}, u32[]{:S(2)}) collective-permute-start(bf16[10,1,16,192]{3,2,1,0:T(8,128)(2,1)S(1)} %get-tuple-element.312), channel_id=1, source_target_pairs={{0,1},{1,2},{2,3},{3,4},{4,5},{5,6},{6,7},{8,9},{9,10},{10,11},{11... | collective-permute-start | bytes 184328 | tf_op jit(solution)/shard_map/while/body/eval_jaxpr/ppermute | solution.py:14
  38.0 3.3 %collective-permute-done.1 = bf16[10,1,16,192]{3,2,1,0:T(8,128)(2,1)S(1)} collective-permute-done((bf16[10,1,16,192]{3,2,1,0:T(8,128)(2,1)S(1)}, bf16[10,1,16,192]{3,2,1,0:T(8,128)(2,1)S(1)}, u32[]{:S(2)}, u32[]{:S(2)}) %collective-permute-start.1) | collective-permute-done | bytes 61472 | tf_op jit(solution)/shard_map/while/body/eval_jaxpr/ppermute | solution.py:14
  41.4 10.9 %conditional.3 = (bf16[8,2,16,192]{3,2,1,0:T(8,128)(2,1)S(1)}) conditional(s32[]{:T(128)} %convert_element_type.53, bf16[8,2,16,192]{3,2,1,0:T(8,128)(2,1)S(1)} %get-tuple-element.308, (bf16[8,2,16,192]{3,2,1,0:T(8,128)(2,1)S(1)}, bf16[10,4,16,192]{3,2,1,0:T(8,128)(2,1)S(1)}, bf16[3,1728,192]{2,1,0:T(8,128)(2,1)}, f32[1,192]{1,0:T(1,128)}) %tuple.80), branch_computations={%region_2.2_spmd, %region_3.3_spmd} | conditional | flops 509902848 | bytes 16879396 | solution.py:75
  41.5 1.4 pad_slice_fusion
  44.3 1.4 concatenate.12
  45.7 1.7 %fusion.2 = f32[256,192]{0,1:T(8,128)S(1)} fusion(bf16[256,1728]{1,0:T(8,128)(2,1)S(1)} %bitcast.40, bf16[3,1728,192]{2,1,0:T(8,128)(2,1)} %get-tuple-element.112), kind=kOutput, calls=%fused_computation.22 | convolution fusion | flops 169869312 | bytes 1966080 | tf_op jit(solution)/shard_map/while/body/eval_jaxpr/cond/branch_1_fun/dot_general | solution.py:55
  48.7 1.7 %convolution_add_fusion.1 = f32[256,192]{0,1:T(8,128)S(1)} fusion(f32[256,192]{0,1:T(8,128)S(1)} %fusion.2, bf16[256,1728]{1,0:T(8,128)(2,1)S(1)} %bitcast.39, bf16[3,1728,192]{2,1,0:T(8,128)(2,1)} %get-tuple-element.112), kind=kOutput, calls=%fused_computation.1 | convolution fusion | flops 169918464 | bytes 2162688 | tf_op jit(solution)/shard_map/while/body/eval_jaxpr/cond/branch_1_fun/dot_general | solution.py:55
  50.4 1.7 %convolution_add_fusion = f32[256,192]{0,1:T(8,128)S(1)} fusion(f32[256,192]{0,1:T(8,128)S(1)} %convolution_add_fusion.1, bf16[256,1728]{1,0:T(8,128)(2,1)S(1)} %bitcast.38, bf16[3,1728,192]{2,1,0:T(8,128)(2,1)} %get-tuple-element.112), kind=kOutput, calls=%fused_computation | convolution fusion | flops 169918464 | bytes 2162688 | tf_op jit(solution)/shard_map/while/body/eval_jaxpr/cond/branch_1_fun/dot_general | solution.py:55
  52.3 4.4 %collective-permute-start.2 = (bf16[8,2,16,192]{3,2,1,0:T(8,128)(2,1)S(1)}, bf16[8,2,16,192]{3,2,1,0:T(8,128)(2,1)S(1)}, u32[]{:S(2)}, u32[]{:S(2)}) collective-permute-start(bf16[8,2,16,192]{3,2,1,0:T(8,128)(2,1)S(1)} %get-tuple-element.359), channel_id=1, source_target_pairs={{0,8},{8,16},{16,24},{1,9},{9,17},{17,25},{2,10},{10,18},{18,26},{... | collective-permute-start | bytes 294920 | tf_op jit(solution)/shard_map/while/body/eval_jaxpr/ppermute | solution.py:25
  56.7 1.6 fusion.28
  58.3 1.5 collective-permute-done.2
  63.6 1.4 slice_select_fusion.2
  65.0 1.9 %collective-permute-start = (bf16[10,1,16,192]{3,2,1,0:T(8,128)(2,1)S(1)}, bf16[10,1,16,192]{3,2,1,0:T(8,128)(2,1)S(1)}, u32[]{:S(2)}, u32[]{:S(2)}) collective-permute-start(bf16[10,1,16,192]{3,2,1,0:T(8,128)(2,1)S(1)} %get-tuple-element.311), channel_id=1, source_target_pairs={{1,0},{2,1},{3,2},{4,3},{5,4},{6,5},{7,6},{9,8},{10,9},{11,10},{12... | collective-permute-start | bytes 184328 | tf_op jit(solution)/shard_map/while/body/eval_jaxpr/ppermute | solution.py:17
  66.9 2.4 %collective-permute-start.1 = (bf16[10,1,16,192]{3,2,1,0:T(8,128)(2,1)S(1)}, bf16[10,1,16,192]{3,2,1,0:T(8,128)(2,1)S(1)}, u32[]{:S(2)}, u32[]{:S(2)}) collective-permute-start(bf16[10,1,16,192]{3,2,1,0:T(8,128)(2,1)S(1)} %get-tuple-element.312), channel_id=1, source_target_pairs={{0,1},{1,2},{2,3},{3,4},{4,5},{5,6},{6,7},{8,9},{9,10},{10,11},{11... | collective-permute-start | bytes 184328 | tf_op jit(solution)/shard_map/while/body/eval_jaxpr/ppermute | solution.py:14
  69.4 3.3 %collective-permute-done.1 = bf16[10,1,16,192]{3,2,1,0:T(8,128)(2,1)S(1)} collective-permute-done((bf16[10,1,16,192]{3,2,1,0:T(8,128)(2,1)S(1)}, bf16[10,1,16,192]{3,2,1,0:T(8,128)(2,1)S(1)}, u32[]{:S(2)}, u32[]{:S(2)}) %collective-permute-start.1) | collective-permute-done | bytes 61472 | tf_op jit(solution)/shard_map/while/body/eval_jaxpr/ppermute | solution.py:14
  72.8 15.3 %collective-permute-start.2 = (bf16[8,2,16,192]{3,2,1,0:T(8,128)(2,1)S(1)}, bf16[8,2,16,192]{3,2,1,0:T(8,128)(2,1)S(1)}, u32[]{:S(2)}, u32[]{:S(2)}) collective-permute-start(bf16[8,2,16,192]{3,2,1,0:T(8,128)(2,1)S(1)} %get-tuple-element.359), channel_id=1, source_target_pairs={{0,8},{8,16},{16,24},{1,9},{9,17},{17,25},{2,10},{10,18},{18,26},{... | collective-permute-start | bytes 294920 | tf_op jit(solution)/shard_map/while/body/eval_jaxpr/ppermute | solution.py:25
  88.1 1.6 fusion.28
  89.7 1.8 %collective-permute-done.2 = bf16[8,2,16,192]{3,2,1,0:T(8,128)(2,1)S(1)} collective-permute-done((bf16[8,2,16,192]{3,2,1,0:T(8,128)(2,1)S(1)}, bf16[8,2,16,192]{3,2,1,0:T(8,128)(2,1)S(1)}, u32[]{:S(2)}, u32[]{:S(2)}) %collective-permute-start.2) | collective-permute-done | bytes 98336 | tf_op jit(solution)/shard_map/while/body/eval_jaxpr/ppermute | solution.py:25
  95.2 1.4 slice_select_fusion.2
  96.7 1.9 %collective-permute-start = (bf16[10,1,16,192]{3,2,1,0:T(8,128)(2,1)S(1)}, bf16[10,1,16,192]{3,2,1,0:T(8,128)(2,1)S(1)}, u32[]{:S(2)}, u32[]{:S(2)}) collective-permute-start(bf16[10,1,16,192]{3,2,1,0:T(8,128)(2,1)S(1)} %get-tuple-element.311), channel_id=1, source_target_pairs={{1,0},{2,1},{3,2},{4,3},{5,4},{6,5},{7,6},{9,8},{10,9},{11,10},{12... | collective-permute-start | bytes 184328 | tf_op jit(solution)/shard_map/while/body/eval_jaxpr/ppermute | solution.py:17
  98.6 2.4 %collective-permute-start.1 = (bf16[10,1,16,192]{3,2,1,0:T(8,128)(2,1)S(1)}, bf16[10,1,16,192]{3,2,1,0:T(8,128)(2,1)S(1)}, u32[]{:S(2)}, u32[]{:S(2)}) collective-permute-start(bf16[10,1,16,192]{3,2,1,0:T(8,128)(2,1)S(1)} %get-tuple-element.312), channel_id=1, source_target_pairs={{0,1},{1,2},{2,3},{3,4},{4,5},{5,6},{6,7},{8,9},{9,10},{10,11},{11... | collective-permute-start | bytes 184328 | tf_op jit(solution)/shard_map/while/body/eval_jaxpr/ppermute | solution.py:14
  101.0 3.3 %collective-permute-done.1 = bf16[10,1,16,192]{3,2,1,0:T(8,128)(2,1)S(1)} collective-permute-done((bf16[10,1,16,192]{3,2,1,0:T(8,128)(2,1)S(1)}, bf16[10,1,16,192]{3,2,1,0:T(8,128)(2,1)S(1)}, u32[]{:S(2)}, u32[]{:S(2)}) %collective-permute-start.1) | collective-permute-done | bytes 61472 | tf_op jit(solution)/shard_map/while/body/eval_jaxpr/ppermute | solution.py:14
  104.4 4.4 %collective-permute-start.2 = (bf16[8,2,16,192]{3,2,1,0:T(8,128)(2,1)S(1)}, bf16[8,2,16,192]{3,2,1,0:T(8,128)(2,1)S(1)}, u32[]{:S(2)}, u32[]{:S(2)}) collective-permute-start(bf16[8,2,16,192]{3,2,1,0:T(8,128)(2,1)S(1)} %get-tuple-element.359), channel_id=1, source_target_pairs={{0,8},{8,16},{16,24},{1,9},{9,17},{17,25},{2,10},{10,18},{18,26},{... | collective-permute-start | bytes 294920 | tf_op jit(solution)/shard_map/while/body/eval_jaxpr/ppermute | solution.py:25
  108.8 1.6 fusion.28
  110.4 1.8 %collective-permute-done.2 = bf16[8,2,16,192]{3,2,1,0:T(8,128)(2,1)S(1)} collective-permute-done((bf16[8,2,16,192]{3,2,1,0:T(8,128)(2,1)S(1)}, bf16[8,2,16,192]{3,2,1,0:T(8,128)(2,1)S(1)}, u32[]{:S(2)}, u32[]{:S(2)}) %collective-permute-start.2) | collective-permute-done | bytes 98336 | tf_op jit(solution)/shard_map/while/body/eval_jaxpr/ppermute | solution.py:25
  116.0 1.4 slice_select_fusion.2
  117.4 1.9 %collective-permute-start = (bf16[10,1,16,192]{3,2,1,0:T(8,128)(2,1)S(1)}, bf16[10,1,16,192]{3,2,1,0:T(8,128)(2,1)S(1)}, u32[]{:S(2)}, u32[]{:S(2)}) collective-permute-start(bf16[10,1,16,192]{3,2,1,0:T(8,128)(2,1)S(1)} %get-tuple-element.311), channel_id=1, source_target_pairs={{1,0},{2,1},{3,2},{4,3},{5,4},{6,5},{7,6},{9,8},{10,9},{11,10},{12... | collective-permute-start | bytes 184328 | tf_op jit(solution)/shard_map/while/body/eval_jaxpr/ppermute | solution.py:17
  119.3 2.4 %collective-permute-start.1 = (bf16[10,1,16,192]{3,2,1,0:T(8,128)(2,1)S(1)}, bf16[10,1,16,192]{3,2,1,0:T(8,128)(2,1)S(1)}, u32[]{:S(2)}, u32[]{:S(2)}) collective-permute-start(bf16[10,1,16,192]{3,2,1,0:T(8,128)(2,1)S(1)} %get-tuple-element.312), channel_id=1, source_target_pairs={{0,1},{1,2},{2,3},{3,4},{4,5},{5,6},{6,7},{8,9},{9,10},{10,11},{11... | collective-permute-start | bytes 184328 | tf_op jit(solution)/shard_map/while/body/eval_jaxpr/ppermute | solution.py:14
  121.8 3.3 %collective-permute-done.1 = bf16[10,1,16,192]{3,2,1,0:T(8,128)(2,1)S(1)} collective-permute-done((bf16[10,1,16,192]{3,2,1,0:T(8,128)(2,1)S(1)}, bf16[10,1,16,192]{3,2,1,0:T(8,128)(2,1)S(1)}, u32[]{:S(2)}, u32[]{:S(2)}) %collective-permute-start.1) | collective-permute-done | bytes 61472 | tf_op jit(solution)/shard_map/while/body/eval_jaxpr/ppermute | solution.py:14
  125.2 12.8 %collective-permute-start.2 = (bf16[8,2,16,192]{3,2,1,0:T(8,128)(2,1)S(1)}, bf16[8,2,16,192]{3,2,1,0:T(8,128)(2,1)S(1)}, u32[]{:S(2)}, u32[]{:S(2)}) collective-permute-start(bf16[8,2,16,192]{3,2,1,0:T(8,128)(2,1)S(1)} %get-tuple-element.359), channel_id=1, source_target_pairs={{0,8},{8,16},{16,24},{1,9},{9,17},{17,25},{2,10},{10,18},{18,26},{... | collective-permute-start | bytes 294920 | tf_op jit(solution)/shard_map/while/body/eval_jaxpr/ppermute | solution.py:25
  138.0 1.6 fusion.28
  139.6 1.8 %collective-permute-done.2 = bf16[8,2,16,192]{3,2,1,0:T(8,128)(2,1)S(1)} collective-permute-done((bf16[8,2,16,192]{3,2,1,0:T(8,128)(2,1)S(1)}, bf16[8,2,16,192]{3,2,1,0:T(8,128)(2,1)S(1)}, u32[]{:S(2)}, u32[]{:S(2)}) %collective-permute-start.2) | collective-permute-done | bytes 98336 | tf_op jit(solution)/shard_map/while/body/eval_jaxpr/ppermute | solution.py:25
  141.4 24.3 %all_to_all.12 = bf16[4,1,4,2,16,192]{5,4,3,2,1,0:T(8,128)(2,1)S(1)} all-to-all(bf16[4,1,4,2,16,192]{5,4,3,2,1,0:T(8,128)(2,1)} %bitcast.43), channel_id=1, replica_groups=mesh['section'=4,'row'=8] {'section'}, dimensions={0} | all-to-all | bytes 393216 | tf_op jit(solution)/shard_map/all_to_all | solution.py:85
  (58 shorter events, 20.8 us)
Async XLA Ops:
  5.2 4.4 %collective-permute-start = (bf16[10,1,16,192]{3,2,1,0:T(8,128)(2,1)S(1)}, bf16[10,1,16,192]{3,2,1,0:T(8,128)(2,1)S(1)}, u32[]{:S(2)}, u32[]{:S(2)}) collective-permute-start(bf16[10,1,16,192]{3,2,1,0:T(8,128)(2,1)S(1)} %get-tuple-element.311), channel_id=1, source_target_pairs={{1,0},{2,1},{3,2},{4,3},{5,4},{6,5},{7,6},{9,8},{10,9},{11,10},{12... | collective-permute-start | bytes 184328 | tf_op jit(solution)/shard_map/while/body/eval_jaxpr/ppermute | solution.py:17
  7.1 5.8 %collective-permute-start.1 = (bf16[10,1,16,192]{3,2,1,0:T(8,128)(2,1)S(1)}, bf16[10,1,16,192]{3,2,1,0:T(8,128)(2,1)S(1)}, u32[]{:S(2)}, u32[]{:S(2)}) collective-permute-start(bf16[10,1,16,192]{3,2,1,0:T(8,128)(2,1)S(1)} %get-tuple-element.312), channel_id=1, source_target_pairs={{0,1},{1,2},{2,3},{3,4},{4,5},{5,6},{6,7},{8,9},{9,10},{10,11},{11... | collective-permute-start | bytes 184328 | tf_op jit(solution)/shard_map/while/body/eval_jaxpr/ppermute | solution.py:14
  20.3 3.5 %copy-start = (f32[1,192]{1,0:T(1,128)S(1)}, f32[1,192]{1,0:T(1,128)}, u32[]{:S(2)}) copy-start(f32[1,192]{1,0:T(1,128)} %get-tuple-element.113) | copy-start | bytes 2308 | tf_op jit(solution)/shard_map/while/body/eval_jaxpr/cond
  23.9 4.6 %collective-permute-start.2 = (bf16[8,2,16,192]{3,2,1,0:T(8,128)(2,1)S(1)}, bf16[8,2,16,192]{3,2,1,0:T(8,128)(2,1)S(1)}, u32[]{:S(2)}, u32[]{:S(2)}) collective-permute-start(bf16[8,2,16,192]{3,2,1,0:T(8,128)(2,1)S(1)} %get-tuple-element.359), channel_id=1, source_target_pairs={{0,8},{8,16},{16,24},{1,9},{9,17},{17,25},{2,10},{10,18},{18,26},{... | collective-permute-start | bytes 294920 | tf_op jit(solution)/shard_map/while/body/eval_jaxpr/ppermute | solution.py:25
  33.7 4.4 %collective-permute-start = (bf16[10,1,16,192]{3,2,1,0:T(8,128)(2,1)S(1)}, bf16[10,1,16,192]{3,2,1,0:T(8,128)(2,1)S(1)}, u32[]{:S(2)}, u32[]{:S(2)}) collective-permute-start(bf16[10,1,16,192]{3,2,1,0:T(8,128)(2,1)S(1)} %get-tuple-element.311), channel_id=1, source_target_pairs={{1,0},{2,1},{3,2},{4,3},{5,4},{6,5},{7,6},{9,8},{10,9},{11,10},{12... | collective-permute-start | bytes 184328 | tf_op jit(solution)/shard_map/while/body/eval_jaxpr/ppermute | solution.py:17
  35.6 5.8 %collective-permute-start.1 = (bf16[10,1,16,192]{3,2,1,0:T(8,128)(2,1)S(1)}, bf16[10,1,16,192]{3,2,1,0:T(8,128)(2,1)S(1)}, u32[]{:S(2)}, u32[]{:S(2)}) collective-permute-start(bf16[10,1,16,192]{3,2,1,0:T(8,128)(2,1)S(1)} %get-tuple-element.312), channel_id=1, source_target_pairs={{0,1},{1,2},{2,3},{3,4},{4,5},{5,6},{6,7},{8,9},{9,10},{10,11},{11... | collective-permute-start | bytes 184328 | tf_op jit(solution)/shard_map/while/body/eval_jaxpr/ppermute | solution.py:14
  48.7 3.5 %copy-start = (f32[1,192]{1,0:T(1,128)S(1)}, f32[1,192]{1,0:T(1,128)}, u32[]{:S(2)}) copy-start(f32[1,192]{1,0:T(1,128)} %get-tuple-element.113) | copy-start | bytes 2308 | tf_op jit(solution)/shard_map/while/body/eval_jaxpr/cond
  52.3 7.5 %collective-permute-start.2 = (bf16[8,2,16,192]{3,2,1,0:T(8,128)(2,1)S(1)}, bf16[8,2,16,192]{3,2,1,0:T(8,128)(2,1)S(1)}, u32[]{:S(2)}, u32[]{:S(2)}) collective-permute-start(bf16[8,2,16,192]{3,2,1,0:T(8,128)(2,1)S(1)} %get-tuple-element.359), channel_id=1, source_target_pairs={{0,8},{8,16},{16,24},{1,9},{9,17},{17,25},{2,10},{10,18},{18,26},{... | collective-permute-start | bytes 294920 | tf_op jit(solution)/shard_map/while/body/eval_jaxpr/ppermute | solution.py:25
  65.0 4.4 %collective-permute-start = (bf16[10,1,16,192]{3,2,1,0:T(8,128)(2,1)S(1)}, bf16[10,1,16,192]{3,2,1,0:T(8,128)(2,1)S(1)}, u32[]{:S(2)}, u32[]{:S(2)}) collective-permute-start(bf16[10,1,16,192]{3,2,1,0:T(8,128)(2,1)S(1)} %get-tuple-element.311), channel_id=1, source_target_pairs={{1,0},{2,1},{3,2},{4,3},{5,4},{6,5},{7,6},{9,8},{10,9},{11,10},{12... | collective-permute-start | bytes 184328 | tf_op jit(solution)/shard_map/while/body/eval_jaxpr/ppermute | solution.py:17
  66.9 5.8 %collective-permute-start.1 = (bf16[10,1,16,192]{3,2,1,0:T(8,128)(2,1)S(1)}, bf16[10,1,16,192]{3,2,1,0:T(8,128)(2,1)S(1)}, u32[]{:S(2)}, u32[]{:S(2)}) collective-permute-start(bf16[10,1,16,192]{3,2,1,0:T(8,128)(2,1)S(1)} %get-tuple-element.312), channel_id=1, source_target_pairs={{0,1},{1,2},{2,3},{3,4},{4,5},{5,6},{6,7},{8,9},{9,10},{10,11},{11... | collective-permute-start | bytes 184328 | tf_op jit(solution)/shard_map/while/body/eval_jaxpr/ppermute | solution.py:14
  72.8 18.6 %collective-permute-start.2 = (bf16[8,2,16,192]{3,2,1,0:T(8,128)(2,1)S(1)}, bf16[8,2,16,192]{3,2,1,0:T(8,128)(2,1)S(1)}, u32[]{:S(2)}, u32[]{:S(2)}) collective-permute-start(bf16[8,2,16,192]{3,2,1,0:T(8,128)(2,1)S(1)} %get-tuple-element.359), channel_id=1, source_target_pairs={{0,8},{8,16},{16,24},{1,9},{9,17},{17,25},{2,10},{10,18},{18,26},{... | collective-permute-start | bytes 294920 | tf_op jit(solution)/shard_map/while/body/eval_jaxpr/ppermute | solution.py:25
  96.7 4.4 %collective-permute-start = (bf16[10,1,16,192]{3,2,1,0:T(8,128)(2,1)S(1)}, bf16[10,1,16,192]{3,2,1,0:T(8,128)(2,1)S(1)}, u32[]{:S(2)}, u32[]{:S(2)}) collective-permute-start(bf16[10,1,16,192]{3,2,1,0:T(8,128)(2,1)S(1)} %get-tuple-element.311), channel_id=1, source_target_pairs={{1,0},{2,1},{3,2},{4,3},{5,4},{6,5},{7,6},{9,8},{10,9},{11,10},{12... | collective-permute-start | bytes 184328 | tf_op jit(solution)/shard_map/while/body/eval_jaxpr/ppermute | solution.py:17
  98.6 5.8 %collective-permute-start.1 = (bf16[10,1,16,192]{3,2,1,0:T(8,128)(2,1)S(1)}, bf16[10,1,16,192]{3,2,1,0:T(8,128)(2,1)S(1)}, u32[]{:S(2)}, u32[]{:S(2)}) collective-permute-start(bf16[10,1,16,192]{3,2,1,0:T(8,128)(2,1)S(1)} %get-tuple-element.312), channel_id=1, source_target_pairs={{0,1},{1,2},{2,3},{3,4},{4,5},{5,6},{6,7},{8,9},{9,10},{10,11},{11... | collective-permute-start | bytes 184328 | tf_op jit(solution)/shard_map/while/body/eval_jaxpr/ppermute | solution.py:14
  104.4 7.8 %collective-permute-start.2 = (bf16[8,2,16,192]{3,2,1,0:T(8,128)(2,1)S(1)}, bf16[8,2,16,192]{3,2,1,0:T(8,128)(2,1)S(1)}, u32[]{:S(2)}, u32[]{:S(2)}) collective-permute-start(bf16[8,2,16,192]{3,2,1,0:T(8,128)(2,1)S(1)} %get-tuple-element.359), channel_id=1, source_target_pairs={{0,8},{8,16},{16,24},{1,9},{9,17},{17,25},{2,10},{10,18},{18,26},{... | collective-permute-start | bytes 294920 | tf_op jit(solution)/shard_map/while/body/eval_jaxpr/ppermute | solution.py:25
  117.4 4.4 %collective-permute-start = (bf16[10,1,16,192]{3,2,1,0:T(8,128)(2,1)S(1)}, bf16[10,1,16,192]{3,2,1,0:T(8,128)(2,1)S(1)}, u32[]{:S(2)}, u32[]{:S(2)}) collective-permute-start(bf16[10,1,16,192]{3,2,1,0:T(8,128)(2,1)S(1)} %get-tuple-element.311), channel_id=1, source_target_pairs={{1,0},{2,1},{3,2},{4,3},{5,4},{6,5},{7,6},{9,8},{10,9},{11,10},{12... | collective-permute-start | bytes 184328 | tf_op jit(solution)/shard_map/while/body/eval_jaxpr/ppermute | solution.py:17
  119.3 5.8 %collective-permute-start.1 = (bf16[10,1,16,192]{3,2,1,0:T(8,128)(2,1)S(1)}, bf16[10,1,16,192]{3,2,1,0:T(8,128)(2,1)S(1)}, u32[]{:S(2)}, u32[]{:S(2)}) collective-permute-start(bf16[10,1,16,192]{3,2,1,0:T(8,128)(2,1)S(1)} %get-tuple-element.312), channel_id=1, source_target_pairs={{0,1},{1,2},{2,3},{3,4},{4,5},{5,6},{6,7},{8,9},{9,10},{10,11},{11... | collective-permute-start | bytes 184328 | tf_op jit(solution)/shard_map/while/body/eval_jaxpr/ppermute | solution.py:14
  125.2 16.2 %collective-permute-start.2 = (bf16[8,2,16,192]{3,2,1,0:T(8,128)(2,1)S(1)}, bf16[8,2,16,192]{3,2,1,0:T(8,128)(2,1)S(1)}, u32[]{:S(2)}, u32[]{:S(2)}) collective-permute-start(bf16[8,2,16,192]{3,2,1,0:T(8,128)(2,1)S(1)} %get-tuple-element.359), channel_id=1, source_target_pairs={{0,8},{8,16},{16,24},{1,9},{9,17},{17,25},{2,10},{10,18},{18,26},{... | collective-permute-start | bytes 294920 | tf_op jit(solution)/shard_map/while/body/eval_jaxpr/ppermute | solution.py:25
where the time goes:
time: 168 us; the launch traced here: 166 us
  starting transfers between devices  59.8 us (36%)
  waiting for transfers between devices  25.1 us (15%)
  blocking collectives  24.3 us (14%)
  other arithmetic  24.1 us (14%)
  local copies, waits for them, and re-layouts  15.8 us (9%)
  matrix products  10.1 us (6%)
  loops' own time  7.08 us (4%)
    ppermute x5, starting transfers between devices, shifted(): lax.ppermute(value, axis, [(source, source + steps) for source in range(f...  38.2 us
    all_to_all x1, blocking collectives, on_device(): lax.all_to_all(finished, 'section', split_axis=0, concat_axis=1, tiled=True)  24.3 us
    ppermute x5, waiting for transfers between devices, with_halo(): lax.ppermute(lax.slice_in_dim(block, block.shape[dim] - width, None, axis...  16.6 us
    ppermute x5, starting transfers between devices, with_halo(): lax.ppermute(lax.slice_in_dim(block, block.shape[dim] - width, None, axis...  12 us
    dot_general x6, matrix products, convolve(): jnp.dot(stacked, taps[delay], preferred_element_type=jnp.float32)  10.1 us
    ppermute x5, starting transfers between devices, with_halo(): lax.ppermute(lax.slice_in_dim(block, 0, width, axis=dim), axis, backward)  9.6 us
    ppermute x5, waiting for transfers between devices, shifted(): lax.ppermute(value, axis, [(source, source + steps) for source in range(f...  8.46 us
    concatenate x6, local copies, waits for them, and re-layouts, convolve(): stacked = jnp.concatenate(pieces, axis=-1).reshape(-1, 9 * chans)  8.15 us
  transfers between devices with their start and end apart: 15, of which 10 were waited for; matrix products, arithmetic and copies ran while one was open for 5% of the time, Pallas kernels for 0%

commit v1 on v0

v1 whole, which is shorter than its diff:
```python
import functools

import jax
import jax.numpy as jnp
from jax import lax
from jax.experimental import pallas as pl
from jax.experimental.pallas import tpu as pltpu
from jax.sharding import PartitionSpec as P

FRAMES = 4
MESH = pl.DeviceIdType.MESH


def layer_kernel(
    sections, places, span, x_hbm, gain_ref, w_hbm, bias_ref, o_ref,
    own, above, below, taps, patches, result,
    load_sem, tap_sem, feature_send, send_sem, recv_sem, done_send, done_recv,
):
    frames, rows, cols, chans = own.shape
    turns = frames // span
    share = o_ref.shape[0]
    area = rows * cols
    layer = lax.axis_index("section")
    place = lax.axis_index("row")
    last = sections - 1
    has_above = place > 0
    has_below = place < places - 1
    is_first = layer == 0
    is_last = layer == last

    tap_copy = pltpu.make_async_copy(w_hbm, taps, tap_sem)
    tap_copy.start()
    own_copy = pltpu.make_async_copy(x_hbm, own, load_sem)

    @pl.when(is_first)
    def _():
        own_copy.start()

    barrier = pltpu.get_barrier_semaphore()

    def greet(section, row):
        pl.semaphore_signal(barrier, inc=1, device_id=(section, row), device_id_type=MESH)

    source = jnp.maximum(layer - 1, 0)

    @pl.when(jnp.logical_not(is_first))
    def _():
        greet(source, place)

    @pl.when(has_above)
    def _():
        greet(source, place - 1)

    @pl.when(has_below)
    def _():
        greet(source, place + 1)

    @pl.when(jnp.logical_not(is_last))
    def _():
        greet(last, place)

    beside = has_above.astype(jnp.int32) + has_below.astype(jnp.int32)
    first = is_first.astype(jnp.int32)
    final = is_last.astype(jnp.int32)
    pl.semaphore_wait(barrier, (1 - final) * (1 + beside) + first * beside + final * last)

    def send(src, dst, send_at, recv_at, section, row):
        return pltpu.make_async_remote_copy(
            src_ref=src, dst_ref=dst, send_sem=send_at, recv_sem=recv_at,
            device_id=(section, row), device_id_type=MESH,
        )

    def feature_above(turn):
        at = pl.ds(turn * span, span)
        return send(
            x_hbm.at[at, 0], below.at[at], feature_send.at[0, turn], recv_sem.at[2, turn], layer, place - 1
        )

    def feature_below(turn):
        at = pl.ds(turn * span, span)
        return send(
            x_hbm.at[at, rows - 1], above.at[at], feature_send.at[1, turn], recv_sem.at[1, turn], layer, place + 1
        )

    def next_own(turn):
        at = pl.ds(turn * span, span)
        return send(result.at[at], own.at[at], send_sem.at[0, turn], recv_sem.at[0, turn], layer + 1, place)

    def next_above(turn):
        at = pl.ds(turn * span, span)
        return send(
            result.at[at, 0], below.at[at], send_sem.at[2, turn], recv_sem.at[2, turn], layer + 1, place - 1
        )

    def next_below(turn):
        at = pl.ds(turn * span, span)
        return send(
            result.at[at, rows - 1], above.at[at], send_sem.at[1, turn], recv_sem.at[1, turn], layer + 1, place + 1
        )

    pieces = share // span

    def keep(turn):
        at = pl.ds(turn * span, span)
        part = lax.rem(turn, pieces)
        return send(
            result.at[at], o_ref.at[pl.ds(part * span, span)], done_send.at[turn], done_recv.at[part],
            turn // pieces, place,
        )

    @pl.when(is_first)
    def _():
        def begin(turn, carry):
            @pl.when(has_above)
            def _():
                feature_above(turn).start()

            @pl.when(has_below)
            def _():
                feature_below(turn).start()

            return carry

        lax.fori_loop(0, turns, begin, 0)

    empty = jnp.zeros(above.shape, above.dtype)

    @pl.when(jnp.logical_not(has_above))
    def _():
        above[...] = empty

    @pl.when(jnp.logical_not(has_below))
    def _():
        below[...] = empty

    patches[0 : 2 * area, :] = jnp.zeros((2 * area, patches.shape[1]), patches.dtype)
    gain = gain_ref[...]
    bias = bias_ref[...]
    wide = span * (rows + 2) * cols
    column = lax.rem(lax.broadcasted_iota(jnp.int32, (wide, chans), 0), cols)

    @pl.when(is_first)
    def _():
        own_copy.wait()

    def advance(turn, carry):
        at = pl.ds(turn * span, span)

        @pl.when(jnp.logical_not(is_first))
        def _():
            next_own(turn).wait_recv()

        @pl.when(has_above)
        def _():
            next_below(turn).wait_recv()

        @pl.when(has_below)
        def _():
            next_above(turn).wait_recv()

        state = own[at].astype(jnp.float32)
        high = above[at].astype(jnp.float32).reshape(span, 1, cols, chans)
        low = below[at].astype(jnp.float32).reshape(span, 1, cols, chans)
        block = jnp.concatenate([high, state, low], axis=1).reshape(wide, chans)
        square = jnp.mean(block * block, axis=-1, keepdims=True)
        scaled = block * lax.rsqrt(square + 1e-06) * gain
        normed = scaled / (1.0 + jnp.exp(-scaled))
        left = jnp.where(column == 0, 0.0, pltpu.roll(normed, 1, 0))
        right = jnp.where(column == cols - 1, 0.0, pltpu.roll(normed, wide - 1, 0))
        shifts = [
            value.astype(jnp.bfloat16).reshape(span, rows + 2, cols, chans)
            for value in (left, normed, right)
        ]
        stacked = jnp.concatenate(
            [
                shifts[dx][:, dy : dy + rows].reshape(span * area, chans)
                for dy in range(3)
                for dx in range(3)
            ],
            axis=-1,
        )
        base = turn * span * area
        patches[pl.ds(pl.multiple_of(base + 2 * area, area), span * area), :] = stacked
        total = state.reshape(span * area, chans) + bias

        @pl.when(turn == 0)
        def _():
            tap_copy.wait()

        for delay in range(3):
            window = patches[pl.ds(pl.multiple_of(base + delay * area, area), span * area), :]
            total = total + jnp.dot(window, taps[delay], preferred_element_type=jnp.float32)
        result[at] = total.astype(jnp.bfloat16).reshape(span, rows, cols, chans)

        @pl.when(jnp.logical_not(is_last))
        def _():
            next_own(turn).start()

            @pl.when(has_above)
            def _():
                next_above(turn).start()

            @pl.when(has_below)
            def _():
                next_below(turn).start()

        @pl.when(jnp.logical_and(is_last, turn // pieces < last))
        def _():
            keep(turn).start()

        return carry

    lax.fori_loop(0, turns, advance, 0)

    @pl.when(is_last)
    def _():
        o_ref[...] = result[pl.ds(frames - share, share)]

        def drain(turn, carry):
            keep(turn).wait_send()
            return carry

        lax.fori_loop(0, last * pieces, drain, 0)

    @pl.when(jnp.logical_not(is_last))
    def _():
        def drain(turn, carry):
            next_own(turn).wait_send()

            @pl.when(has_above)
            def _():
                next_above(turn).wait_send()

            @pl.when(has_below)
            def _():
                next_below(turn).wait_send()

            return carry

        lax.fori_loop(0, turns, drain, 0)

        def arrive(part, carry):
            keep(part).wait_recv()
            return carry

        lax.fori_loop(0, pieces, arrive, 0)

    @pl.when(is_first)
    def _():
        def drain(turn, carry):
            @pl.when(has_above)
            def _():
                feature_above(turn).wait_send()

            @pl.when(has_below)
            def _():
                feature_below(turn).wait_send()

            return carry

        lax.fori_loop(0, turns, drain, 0)


def on_device(features, norm_gain, conv_weight, conv_bias):
    sections = lax.axis_size("section")
    places = lax.axis_size("row")
    frames, rows, cols, chans = features.shape
    share = frames // sections
    span = min(FRAMES, share)
    turns = frames // span
    taps = conv_weight[0].reshape(3, 9 * chans, chans)
    vmem = pl.BlockSpec(memory_space=pltpu.VMEM)
    anywhere = pl.BlockSpec(memory_space=pl.ANY)
    dma = pltpu.SemaphoreType.DMA
    return pl.pallas_call(
        functools.partial(layer_kernel, sections, places, span),
        out_shape=jax.ShapeDtypeStruct((share, rows, cols, chans), jnp.bfloat16),
        in_specs=[anywhere, vmem, anywhere, vmem],
        out_specs=vmem,
        scratch_shapes=[
            pltpu.VMEM((frames, rows, cols, chans), jnp.bfloat16),
            pltpu.VMEM((frames, cols, chans), jnp.bfloat16),
            pltpu.VMEM((frames, cols, chans), jnp.bfloat16),
            pltpu.VMEM((3, 9 * chans, chans), jnp.bfloat16),
            pltpu.VMEM(((frames + 2) * rows * cols, 9 * chans), jnp.bfloat16),
            pltpu.VMEM((frames, rows, cols, chans), jnp.bfloat16),
            dma, dma, dma((2, turns)), dma((3, turns)), dma((3, turns)), dma((turns,)), dma((share // span,)),
        ],
        compiler_params=pltpu.CompilerParams(
            collective_id=0, has_side_effects=True, vmem_limit_bytes=40 * 1024 * 1024
        ),
    )(features, norm_gain, taps, conv_bias)


def solution(mesh):
    in_specs = (
        P(None, "row", None, None),
        P("section", None),
        P("section", None, None, None, None, None),
        P("section", None),
    )
    out_specs = P("section", "row", None, None)
    return jax.shard_map(
        on_device, mesh=mesh, in_specs=in_specs, out_specs=out_specs, check_vma=False
    )
```

time: 168 us -> 37.4 us (0.22)
  the two profiles are of different devices: /device:TPU:2 before, /device:TPU:20 now
where the time goes in v1:
time: 37.4 us; the launch traced here: 37.2 us
  Pallas kernels  32.5 us (87%)
  local copies, waits for them, and re-layouts  4.69 us (13%)
    pallas_call x1, Pallas kernels, on_device(): pl.pallas_call(functools.partial(layer_kernel, sections, places, span), o...  32.5 us
    unnamed x9, local copies, waits for them, and re-layouts  4.69 us

profile of v1, /device:TPU:20, one launch (start us, length us, event | category | flops | bytes accessed | tf_op | source)
XLA Modules:
  0.0 37.2 jit_solution(17973930661615704238)
XLA Ops:
  0.0 0.0 copy-start
  0.0 1.7 %copy-done = bf16[1,3,3,3,192,192]{5,4,3,2,1,0:T(8,128)(2,1)S(1)} copy-done((bf16[1,3,3,3,192,192]{5,4,3,2,1,0:T(8,128)(2,1)S(1)}, bf16[1,3,3,3,192,192]{5,4,3,2,1,0:T(8,128)(2,1)}, u32[]{:S(2)}) %copy-start) | copy-done | bytes 1990680
  1.8 0.0 copy-start.1
  1.8 0.9 %copy-done.1 = bf16[16,2,16,192]{3,2,1,0:T(8,128)(2,1)S(1)} copy-done((bf16[16,2,16,192]{3,2,1,0:T(8,128)(2,1)S(1)}, bf16[16,2,16,192]{3,2,1,0:T(8,128)(2,1)}, u32[]{:S(2)}) %copy-start.1) | copy-done | bytes 196632
  2.7 0.0 copy-start.2
  2.7 0.7 %copy-done.2 = f32[1,192]{1,0:T(1,128)S(1)} copy-done((f32[1,192]{1,0:T(1,128)S(1)}, f32[1,192]{1,0:T(1,128)}, u32[]{:S(2)}) %copy-start.2) | copy-done | bytes 792
  3.4 0.0 copy-start.3
  3.4 0.7 %copy-done.3 = f32[1,192]{1,0:T(1,128)S(1)} copy-done((f32[1,192]{1,0:T(1,128)S(1)}, f32[1,192]{1,0:T(1,128)}, u32[]{:S(2)}) %copy-start.3) | copy-done | bytes 792
  4.1 32.5 %shard_map.46 = bf16[4,2,16,192]{3,2,1,0:T(8,128)(2,1)S(1)} custom-call(bf16[16,2,16,192]{3,2,1,0:T(8,128)(2,1)S(1)} %copy-done.1, f32[1,192]{1,0:T(1,128)S(1)} %copy-done.2, bf16[3,1728,192]{2,1,0:T(8,128)(2,1)S(1)} %bitcast.1, f32[1,192]{1,0:T(1,128)S(1)} %copy-done.3), custom_call_target="tpu_custom_call" | custom-call | tf_op jit(solution)/shard_map/pallas_call | solution.py:275
  36.6 0.6 %copy.6 = bf16[4,2,16,192]{3,2,1,0:T(8,128)(2,1)} copy(bf16[4,2,16,192]{3,2,1,0:T(8,128)(2,1)S(1)} %shard_map.46) | data formatting | bytes 98304
Async XLA Ops:
  0.0 1.7 %copy-start = (bf16[1,3,3,3,192,192]{5,4,3,2,1,0:T(8,128)(2,1)S(1)}, bf16[1,3,3,3,192,192]{5,4,3,2,1,0:T(8,128)(2,1)}, u32[]{:S(2)}) copy-start(bf16[1,3,3,3,192,192]{5,4,3,2,1,0:T(8,128)(2,1)} %param.6) | copy-start | bytes 5971972
  1.8 0.9 %copy-start.1 = (bf16[16,2,16,192]{3,2,1,0:T(8,128)(2,1)S(1)}, bf16[16,2,16,192]{3,2,1,0:T(8,128)(2,1)}, u32[]{:S(2)}) copy-start(bf16[16,2,16,192]{3,2,1,0:T(8,128)(2,1)} %x_hbm.1) | copy-start | bytes 589828
  2.7 0.7 %copy-start.2 = (f32[1,192]{1,0:T(1,128)S(1)}, f32[1,192]{1,0:T(1,128)}, u32[]{:S(2)}) copy-start(f32[1,192]{1,0:T(1,128)} %gain_ref.1) | copy-start | bytes 2308
  3.4 0.7 %copy-start.3 = (f32[1,192]{1,0:T(1,128)S(1)}, f32[1,192]{1,0:T(1,128)}, u32[]{:S(2)}) copy-start(f32[1,192]{1,0:T(1,128)} %bias_ref.1) | copy-start | bytes 2308

commit v2 on v1

v2 whole, which is shorter than its diff:
```python
import functools

import jax
import jax.numpy as jnp
from jax import lax
from jax.experimental import pallas as pl
from jax.experimental.pallas import tpu as pltpu
from jax.sharding import PartitionSpec as P

FRAMES = 2
LANES = 128
MESH = pl.DeviceIdType.MESH


def layer_kernel(
    sections, places, span, x_hbm, gain_hbm, w_hbm, bias_hbm, o_ref,
    features, own, above, below, gain_ref, bias_ref, taps, patches, result, finished,
    load_sem, feature_send, edge_send, edge_recv, next_send, next_recv, done_send, done_recv,
):
    frames, rows, cols, chans = features.shape
    turns = frames // span
    share = o_ref.shape[0]
    pieces = share // span
    area = rows * cols
    layer = lax.axis_index("section")
    place = lax.axis_index("row")
    last = sections - 1
    has_above = place > 0
    has_below = place < places - 1
    is_first = layer == 0
    is_last = layer == last

    own_copy = pltpu.make_async_copy(x_hbm, features, load_sem.at[0])
    gain_copy = pltpu.make_async_copy(gain_hbm, gain_ref, load_sem.at[1])
    bias_copy = pltpu.make_async_copy(bias_hbm, bias_ref, load_sem.at[2])
    tap_copy = pltpu.make_async_copy(w_hbm, taps, load_sem.at[3])

    @pl.when(is_first)
    def _():
        own_copy.start()

    gain_copy.start()
    bias_copy.start()
    tap_copy.start()

    barrier = pltpu.get_barrier_semaphore()

    def greet(section, row):
        pl.semaphore_signal(barrier, inc=1, device_id=(section, row), device_id_type=MESH)

    source = jnp.maximum(layer - 1, 0)

    @pl.when(jnp.logical_not(is_first))
    def _():
        greet(source, place)

    @pl.when(has_above)
    def _():
        greet(source, place - 1)

    @pl.when(has_below)
    def _():
        greet(source, place + 1)

    @pl.when(jnp.logical_not(is_last))
    def _():
        greet(last, place)

    def pack(ref, at, value):
        upper, lower = value[:, 0], value[:, 1]
        ref[at, 0:cols, :] = upper[..., :LANES]
        ref[at, cols : 2 * cols, :] = jnp.concatenate([upper[..., LANES:], lower[..., LANES:]], axis=-1)
        ref[at, 2 * cols : 3 * cols, :] = lower[..., :LANES]

    empty = jnp.zeros(above.shape, above.dtype)

    @pl.when(jnp.logical_not(has_above))
    def _():
        above[...] = empty

    @pl.when(jnp.logical_not(has_below))
    def _():
        below[...] = empty

    patches[0 : 2 * area, :] = jnp.zeros((2 * area, patches.shape[1]), patches.dtype)
    wide = span * (rows + 2) * cols
    column = lax.rem(lax.broadcasted_iota(jnp.int32, (wide, chans), 0), cols)

    @pl.when(is_first)
    def _():
        own_copy.wait()
        pack(own, slice(None), features[...])

    beside = has_above.astype(jnp.int32) + has_below.astype(jnp.int32)
    first = is_first.astype(jnp.int32)
    final = is_last.astype(jnp.int32)
    pl.semaphore_wait(barrier, (1 - final) * (1 + beside) + first * beside + final * last)

    def stretch(turn):
        return pl.ds(turn * span, span)

    def send(src, dst, send_at, recv_at, section, row):
        return pltpu.make_async_remote_copy(
            src_ref=src, dst_ref=dst, send_sem=send_at, recv_sem=recv_at,
            device_id=(section, row), device_id_type=MESH,
        )

    def to_above(turn, src, sems, section):
        at = stretch(turn)
        return send(
            src.at[at, 0 : 2 * cols], below.at[at], sems.at[0, turn], edge_recv.at[0, turn], section, place - 1
        )

    def to_below(turn, src, sems, section):
        at = stretch(turn)
        return send(
            src.at[at, cols : 3 * cols], above.at[at], sems.at[1, turn], edge_recv.at[1, turn], section, place + 1
        )

    def own_above(turn):
        return to_above(turn, own, feature_send, layer)

    def own_below(turn):
        return to_below(turn, own, feature_send, layer)

    def next_above(turn):
        return to_above(turn, result, edge_send, layer + 1)

    def next_below(turn):
        return to_below(turn, result, edge_send, layer + 1)

    def to_next(turn):
        at = stretch(turn)
        return send(result.at[at], own.at[at], next_send.at[turn], next_recv.at[turn], layer + 1, place)

    def to_keeper(turn):
        part = lax.rem(turn, pieces)
        return send(
            finished.at[stretch(turn)], o_ref.at[stretch(part)], done_send.at[turn], done_recv.at[part],
            turn // pieces, place,
        )

    @pl.when(is_first)
    def _():
        def begin(turn, carry):
            @pl.when(has_above)
            def _():
                own_above(turn).start()

            @pl.when(has_below)
            def _():
                own_below(turn).start()

            return carry

        lax.fori_loop(0, turns, begin, 0)

    gain_copy.wait()
    bias_copy.wait()
    gain = gain_ref[...]
    bias = bias_ref[...]
    rest = chans - LANES

    def advance(turn, carry):
        at = stretch(turn)

        @pl.when(jnp.logical_not(is_first))
        def _():
            to_next(turn).wait_recv()

        @pl.when(has_above)
        def _():
            own_below(turn).wait_recv()

        @pl.when(has_below)
        def _():
            own_above(turn).wait_recv()

        def image_row(low, high):
            return jnp.concatenate([low, high], axis=-1).reshape(span, 1, cols, chans)

        held = own[at].astype(jnp.float32)
        over = above[at].astype(jnp.float32)
        under = below[at].astype(jnp.float32)
        mixed = held[:, cols : 2 * cols]
        upper = image_row(held[:, 0:cols], mixed[..., :rest])
        lower = image_row(held[:, 2 * cols :], mixed[..., rest:])
        high = image_row(over[:, cols:], over[:, 0:cols, rest:])
        low = image_row(under[:, 0:cols], under[:, cols:, :rest])
        block = jnp.concatenate([high, upper, lower, low], axis=1)
        state = block[:, 1:3].reshape(span * area, chans)
        block = block.reshape(wide, chans)
        square = jnp.mean(block * block, axis=-1, keepdims=True)
        scaled = block * lax.rsqrt(square + 1e-06) * gain
        normed = scaled / (1.0 + jnp.exp(-scaled))
        left = jnp.where(column == 0, 0.0, pltpu.roll(normed, 1, 0))
        right = jnp.where(column == cols - 1, 0.0, pltpu.roll(normed, wide - 1, 0))
        shifts = [
            value.astype(jnp.bfloat16).reshape(span, rows + 2, cols, chans)
            for value in (left, normed, right)
        ]
        stacked = jnp.concatenate(
            [
                shifts[dx][:, dy : dy + rows].reshape(span * area, chans)
                for dy in range(3)
                for dx in range(3)
            ],
            axis=-1,
        )
        base = turn * span * area
        patches[pl.ds(pl.multiple_of(base + 2 * area, area), span * area), :] = stacked
        total = state + bias

        @pl.when(turn == 0)
        def _():
            tap_copy.wait()

        for delay in range(3):
            window = patches[pl.ds(pl.multiple_of(base + delay * area, area), span * area), :]
            total = total + jnp.dot(window, taps[delay], preferred_element_type=jnp.float32)
        output = total.astype(jnp.bfloat16).reshape(span, rows, cols, chans)

        @pl.when(jnp.logical_not(is_last))
        def _():
            pack(result, at, output)
            to_next(turn).start()

            @pl.when(has_above)
            def _():
                next_above(turn).start()

            @pl.when(has_below)
            def _():
                next_below(turn).start()

        @pl.when(is_last)
        def _():
            finished[at] = output

            @pl.when(turn // pieces < last)
            def _():
                to_keeper(turn).start()

        return carry

    lax.fori_loop(0, turns, advance, 0)

    @pl.when(is_last)
    def _():
        o_ref[...] = finished[pl.ds(frames - share, share)]

        def drain(turn, carry):
            to_keeper(turn).wait_send()
            return carry

        lax.fori_loop(0, last * pieces, drain, 0)

    def drain(turn, carry):
        @pl.when(is_first & has_above)
        def _():
            own_above(turn).wait_send()

        @pl.when(is_first & has_below)
        def _():
            own_below(turn).wait_send()

        @pl.when(jnp.logical_not(is_last))
        def _():
            to_next(turn).wait_send()

            @pl.when(has_above)
            def _():
                next_above(turn).wait_send()

            @pl.when(has_below)
            def _():
                next_below(turn).wait_send()

        return carry

    lax.fori_loop(0, turns, drain, 0)

    @pl.when(jnp.logical_not(is_last))
    def _():
        def arrive(part, carry):
            to_keeper(part).wait_recv()
            return carry

        lax.fori_loop(0, pieces, arrive, 0)


def on_device(features, norm_gain, conv_weight, conv_bias):
    sections = lax.axis_size("section")
    places = lax.axis_size("row")
    frames, rows, cols, chans = features.shape
    share = frames // sections
    span = min(FRAMES, share)
    turns = frames // span
    taps = conv_weight[0].reshape(3, 9 * chans, chans)
    anywhere = pl.BlockSpec(memory_space=pl.ANY)
    dma = pltpu.SemaphoreType.DMA
    half = jnp.bfloat16
    return pl.pallas_call(
        functools.partial(layer_kernel, sections, places, span),
        out_shape=jax.ShapeDtypeStruct((share, rows, cols, chans), half),
        in_specs=[anywhere] * 4,
        out_specs=pl.BlockSpec(memory_space=pltpu.VMEM),
        scratch_shapes=[
            pltpu.VMEM((frames, rows, cols, chans), half),
            pltpu.VMEM((frames, 3 * cols, LANES), half),
            pltpu.VMEM((frames, 2 * cols, LANES), half),
            pltpu.VMEM((frames, 2 * cols, LANES), half),
            pltpu.VMEM(norm_gain.shape, jnp.float32),
            pltpu.VMEM(conv_bias.shape, jnp.float32),
            pltpu.VMEM((3, 9 * chans, chans), half),
            pltpu.VMEM(((frames + 2) * rows * cols, 9 * chans), half),
            pltpu.VMEM((frames, 3 * cols, LANES), half),
            pltpu.VMEM((frames, rows, cols, chans), half),
            dma((4,)), dma((2, turns)), dma((2, turns)), dma((2, turns)), dma((turns,)), dma((turns,)),
            dma((turns,)), dma((share // span,)),
        ],
        compiler_params=pltpu.CompilerParams(
            collective_id=0, has_side_effects=True, vmem_limit_bytes=60 * 1024 * 1024
        ),
    )(features, norm_gain, taps, conv_bias)


def solution(mesh):
    in_specs = (
        P(None, "row", None, None),
        P("section", None),
        P("section", None, None, None, None, None),
        P("section", None),
    )
    out_specs = P("section", "row", None, None)
    return jax.shard_map(
        on_device, mesh=mesh, in_specs=in_specs, out_specs=out_specs, check_vma=False
    )
```

time: 37.4 us -> 30.8 us (0.82)
  Pallas kernels: 32.5 us -> 29.1 us
  local copies, waits for them, and re-layouts: 4.69 us -> 1.47 us
    pallas_call x1, Pallas kernels: 32.5 us -> 29.1 us  [on_device(): pl.pallas_call(functools.partial(layer_kernel, sections, places, span), o...]
    unnamed x9 -> x1, local copies, waits for them, and re-layouts: 4.69 us -> 1.47 us
where the time goes in v2:
time: 30.8 us; the launch traced here: 30.6 us
  Pallas kernels  29.1 us (94%)
  local copies, waits for them, and re-layouts  1.47 us (5%)
    pallas_call x1, Pallas kernels, on_device(): pl.pallas_call(functools.partial(layer_kernel, sections, places, span), o...  29.1 us
    unnamed x1, local copies, waits for them, and re-layouts  1.47 us

profile of v2, /device:TPU:20, one launch (start us, length us, event | category | flops | bytes accessed | tf_op | source)
XLA Modules:
  0.0 30.6 jit_solution(12739585877599710365)
XLA Ops:
  0.0 29.1 %shard_map.46 = bf16[4,2,16,192]{3,2,1,0:T(8,128)(2,1)} custom-call(bf16[16,2,16,192]{3,2,1,0:T(8,128)(2,1)} %x_hbm.1, f32[1,192]{1,0:T(1,128)} %gain_hbm.1, bf16[3,1728,192]{2,1,0:T(8,128)(2,1)} %bitcast.1, f32[1,192]{1,0:T(1,128)} %bias_hbm.1), custom_call_target="tpu_custom_call" | custom-call | tf_op jit(solution)/shard_map/pallas_call | solution.py:303
  29.1 1.5 %copy.6 = bf16[4,2,16,192]{3,2,1,0:T(8,128)(2,1)} copy(bf16[4,2,16,192]{3,2,1,0:T(8,128)(2,1)} %shard_map.46) | data formatting | bytes 98304

commit v3 on v2

--- a/solution.py
+++ b/solution.py
@@ -66,11 +66,16 @@
     def _():
         greet(last, place)
 
-    def pack(ref, at, value):
-        upper, lower = value[:, 0], value[:, 1]
-        ref[at, 0:cols, :] = upper[..., :LANES]
-        ref[at, cols : 2 * cols, :] = jnp.concatenate([upper[..., LANES:], lower[..., LANES:]], axis=-1)
-        ref[at, 2 * cols : 3 * cols, :] = lower[..., :LANES]
+    def pack(first, second):
+        middle = jnp.concatenate([first[..., LANES:], second[..., LANES:]], axis=-1)
+        return jnp.concatenate([first[..., :LANES], middle, second[..., :LANES]], axis=-2)
+
+    def unpack(value):
+        middle = value[..., cols : 2 * cols, :]
+        rest = chans - LANES
+        first = jnp.concatenate([value[..., 0:cols, :], middle[..., :rest]], axis=-1)
+        second = jnp.concatenate([value[..., 2 * cols :, :], middle[..., rest:]], axis=-1)
+        return jnp.stack([first, second])
 
     empty = jnp.zeros(above.shape, above.dtype)
 
@@ -82,14 +87,15 @@
     def _():
         below[...] = empty
 
-    patches[0 : 2 * area, :] = jnp.zeros((2 * area, patches.shape[1]), patches.dtype)
+    patches[:, 0:2] = jnp.zeros((3, 2) + patches.shape[2:], patches.dtype)
     wide = span * (rows + 2) * cols
     column = lax.rem(lax.broadcasted_iota(jnp.int32, (wide, chans), 0), cols)
 
     @pl.when(is_first)
     def _():
         own_copy.wait()
-        pack(own, slice(None), features[...])
+        value = features[...].reshape(turns, span, rows, cols, chans)
+        own[...] = pack(value[:, 0], value[:, 1])
 
     beside = has_above.astype(jnp.int32) + has_below.astype(jnp.int32)
     first = is_first.astype(jnp.int32)
@@ -108,13 +114,13 @@
     def to_above(turn, src, sems, section):
         at = stretch(turn)
         return send(
-            src.at[at, 0 : 2 * cols], below.at[at], sems.at[0, turn], edge_recv.at[0, turn], section, place - 1
+            src.at[turn, 0], below.at[turn], sems.at[0, turn], edge_recv.at[0, turn], section, place - 1
         )
 
     def to_below(turn, src, sems, section):
         at = stretch(turn)
         return send(
-            src.at[at, cols : 3 * cols], above.at[at], sems.at[1, turn], edge_recv.at[1, turn], section, place + 1
+            src.at[turn, rows - 1], above.at[turn], sems.at[1, turn], edge_recv.at[1, turn], section, place + 1
         )
 
     def own_above(turn):
@@ -131,7 +137,7 @@
 
     def to_next(turn):
         at = stretch(turn)
-        return send(result.at[at], own.at[at], next_send.at[turn], next_recv.at[turn], layer + 1, place)
+        return send(result.at[turn], own.at[turn], next_send.at[turn], next_recv.at[turn], layer + 1, place)
 
     def to_keeper(turn):
         part = lax.rem(turn, pieces)
@@ -157,13 +163,23 @@
 
     gain_copy.wait()
     bias_copy.wait()
+    tap_copy.wait()
     gain = gain_ref[...]
     bias = bias_ref[...]
-    rest = chans - LANES
 
     def advance(turn, carry):
         at = stretch(turn)
 
+        def mixed(delay):
+            out = jnp.zeros((span * area, chans), jnp.float32)
+            for dy in range(3):
+                for dx in range(3):
+                    window = patches[dx, pl.ds(turn * span + delay, span), dy : dy + rows].reshape(span * area, chans)
+                    out = out + jnp.dot(window, taps[delay, dy, dx], preferred_element_type=jnp.float32)
+            return out
+
+        partial = mixed(0) + bias
+
         @pl.when(jnp.logical_not(is_first))
         def _():
             to_next(turn).wait_recv()
@@ -176,18 +192,8 @@
         def _():
             own_above(turn).wait_recv()
 
-        def image_row(low, high):
-            return jnp.concatenate([low, high], axis=-1).reshape(span, 1, cols, chans)
-
-        held = own[at].astype(jnp.float32)
-        over = above[at].astype(jnp.float32)
-        under = below[at].astype(jnp.float32)
-        mixed = held[:, cols : 2 * cols]
-        upper = image_row(held[:, 0:cols], mixed[..., :rest])
-        lower = image_row(held[:, 2 * cols :], mixed[..., rest:])
-        high = image_row(over[:, cols:], over[:, 0:cols, rest:])
-        low = image_row(under[:, 0:cols], under[:, cols:, :rest])
-        block = jnp.concatenate([high, upper, lower, low], axis=1)
+        block = jnp.concatenate([above[turn][None], own[turn], below[turn][None]], axis=0)
+        block = unpack(block).astype(jnp.float32)
         state = block[:, 1:3].reshape(span * area, chans)
         block = block.reshape(wide, chans)
         square = jnp.mean(block * block, axis=-1, keepdims=True)
@@ -199,30 +205,14 @@
             value.astype(jnp.bfloat16).reshape(span, rows + 2, cols, chans)
             for value in (left, normed, right)
         ]
-        stacked = jnp.concatenate(
-            [
-                shifts[dx][:, dy : dy + rows].reshape(span * area, chans)
-                for dy in range(3)
-                for dx in range(3)
-            ],
-            axis=-1,
-        )
-        base = turn * span * area
-        patches[pl.ds(pl.multiple_of(base + 2 * area, area), span * area), :] = stacked
-        total = state + bias
-
-        @pl.when(turn == 0)
-        def _():
-            tap_copy.wait()
-
-        for delay in range(3):
-            window = patches[pl.ds(pl.multiple_of(base + delay * area, area), span * area), :]
-            total = total + jnp.dot(window, taps[delay], preferred_element_type=jnp.float32)
+        for dx in range(3):
+            patches[dx, pl.ds(turn * span + 2, span)] = shifts[dx]
+        total = state + (partial + mixed(1) + mixed(2))
         output = total.astype(jnp.bfloat16).reshape(span, rows, cols, chans)
 
         @pl.when(jnp.logical_not(is_last))
         def _():
-            pack(result, at, output)
+            result[turn] = pack(output[0], output[1])
             to_next(turn).start()
 
             @pl.when(has_above)
@@ -294,9 +284,9 @@
     places = lax.axis_size("row")
     frames, rows, cols, chans = features.shape
     share = frames // sections
-    span = min(FRAMES, share)
+    span = FRAMES
     turns = frames // span
-    taps = conv_weight[0].reshape(3, 9 * chans, chans)
+    taps = conv_weight[0]
     anywhere = pl.BlockSpec(memory_space=pl.ANY)
     dma = pltpu.SemaphoreType.DMA
     half = jnp.bfloat16
@@ -307,14 +297,14 @@
         out_specs=pl.BlockSpec(memory_space=pltpu.VMEM),
         scratch_shapes=[
             pltpu.VMEM((frames, rows, cols, chans), half),
-            pltpu.VMEM((frames, 3 * cols, LANES), half),
-            pltpu.VMEM((frames, 2 * cols, LANES), half),
-            pltpu.VMEM((frames, 2 * cols, LANES), half),
+            pltpu.VMEM((turns, rows, 3 * cols, LANES), half),
+            pltpu.VMEM((turns, 3 * cols, LANES), half),
+            pltpu.VMEM((turns, 3 * cols, LANES), half),
             pltpu.VMEM(norm_gain.shape, jnp.float32),
             pltpu.VMEM(conv_bias.shape, jnp.float32),
-            pltpu.VMEM((3, 9 * chans, chans), half),
-            pltpu.VMEM(((frames + 2) * rows * cols, 9 * chans), half),
-            pltpu.VMEM((frames, 3 * cols, LANES), half),
+            pltpu.VMEM((3, 3, 3, chans, chans), half),
+            pltpu.VMEM((3, frames + 2, rows + 2, cols, chans), half),
+            pltpu.VMEM((turns, rows, 3 * cols, LANES), half),
             pltpu.VMEM((frames, rows, cols, chans), half),
             dma((4,)), dma((2, turns)), dma((2, turns)), dma((2, turns)), dma((turns,)), dma((turns,)),
             dma((turns,)), dma((share // span,)),

time: 30.8 us -> 28.7 us (0.932)
  Pallas kernels: 29.1 us -> 27 us
    pallas_call x1, Pallas kernels: 29.1 us -> 27 us  [on_device(): pl.pallas_call(functools.partial(layer_kernel, sections, places, span), o...]
where the time goes in v3:
time: 28.7 us; the launch traced here: 28.5 us
  Pallas kernels  27 us (94%)
  local copies, waits for them, and re-layouts  1.47 us (5%)
    pallas_call x1, Pallas kernels, on_device(): pl.pallas_call(functools.partial(layer_kernel, sections, places, span), o...  27 us
    unnamed x1, local copies, waits for them, and re-layouts  1.47 us

profile of v3, /device:TPU:20, one launch (start us, length us, event | category | flops | bytes accessed | tf_op | source)
XLA Modules:
  0.0 28.5 jit_solution(14250571567922665102)
XLA Ops:
  0.0 27.0 %shard_map.46 = bf16[4,2,16,192]{3,2,1,0:T(8,128)(2,1)} custom-call(bf16[16,2,16,192]{3,2,1,0:T(8,128)(2,1)} %x_hbm.1, f32[1,192]{1,0:T(1,128)} %gain_hbm.1, bf16[3,3,3,192,192]{4,3,2,1,0:T(8,128)(2,1)} %bitcast.1, f32[1,192]{1,0:T(1,128)} %bias_hbm.1), custom_call_target="tpu_custom_call" | custom-call | tf_op jit(solution)/shard_map/pallas_call | solution.py:293
  27.0 1.5 %copy.6 = bf16[4,2,16,192]{3,2,1,0:T(8,128)(2,1)} copy(bf16[4,2,16,192]{3,2,1,0:T(8,128)(2,1)} %shard_map.46) | data formatting | bytes 98304

commit v4 on v3

--- a/solution.py
+++ b/solution.py
@@ -213,15 +213,15 @@
         @pl.when(jnp.logical_not(is_last))
         def _():
             result[turn] = pack(output[0], output[1])
+            @pl.when(has_above)
+            def _():
+                next_above(turn).start()
+
+            @pl.when(has_below)
+            def _():
+                next_below(turn).start()
+
             to_next(turn).start()
-
-            @pl.when(has_above)
-            def _():
-                next_above(turn).start()
-
-            @pl.when(has_below)
-            def _():
-                next_below(turn).start()
 
         @pl.when(is_last)
         def _():

time: 28.7 us -> 28.4 us (0.990)
  no operation moved by 1% of the time
where the time goes in v4:
time: 28.4 us; the launch traced here: 28.3 us
  Pallas kernels  26.8 us (94%)
  local copies, waits for them, and re-layouts  1.47 us (5%)
    pallas_call x1, Pallas kernels, on_device(): pl.pallas_call(functools.partial(layer_kernel, sections, places, span), o...  26.8 us
    unnamed x1, local copies, waits for them, and re-layouts  1.47 us

profile of v4, /device:TPU:20, one launch (start us, length us, event | category | flops | bytes accessed | tf_op | source)
XLA Modules:
  0.0 28.3 jit_solution(1876192347497601314)
XLA Ops:
  0.0 26.8 %shard_map.46 = bf16[4,2,16,192]{3,2,1,0:T(8,128)(2,1)} custom-call(bf16[16,2,16,192]{3,2,1,0:T(8,128)(2,1)} %x_hbm.1, f32[1,192]{1,0:T(1,128)} %gain_hbm.1, bf16[3,3,3,192,192]{4,3,2,1,0:T(8,128)(2,1)} %bitcast.1, f32[1,192]{1,0:T(1,128)} %bias_hbm.1), custom_call_target="tpu_custom_call" | custom-call | tf_op jit(solution)/shard_map/pallas_call | solution.py:293
  26.8 1.5 %copy.6 = bf16[4,2,16,192]{3,2,1,0:T(8,128)(2,1)} copy(bf16[4,2,16,192]{3,2,1,0:T(8,128)(2,1)} %shard_map.46) | data formatting | bytes 98304
